TPU v7x, 256 devices: a whole 4x4x8 slice. The times are simulated.
256 devices in a mesh: grp: 8 (over y, core), row: 32 (over z, x).
Axes of the slice: x: 4, y: 4, z: 8, core: 2. Of those that a mesh axis runs over, the one named last changes fastest.
Arguments:
- features: bfloat16 [524288, 256], P(('grp', 'row')), may hold values from -6 to 6
- cotangent: bfloat16 [524288, 256], P(('grp', 'row')), may hold values from -6 to 6
- self_weight: bfloat16 [256, 256], replicated, may hold values from -0.375 to 0.375
- neighbor_weight: bfloat16 [256, 256], replicated, may hold values from -0.375 to 0.375
- tile_values: bfloat16 [256, 64, 128, 128], P(('grp', 'row')), may hold values from 0 to 1
- tile_index: int32 [256, 64, 2], P(('grp', 'row')), may hold values from 0 to 15
- hub_adjacency: bfloat16 [524288, 1024], P(('grp', 'row')), may hold values from 0 to 1
- hub_owner: int32 [8, 8], P('grp'), may hold values from 0 to 31
- send_rows: int32 [256, 8, 64], P(('grp', 'row')), may hold values from 0 to 2047
- cut_adjacency: bfloat16 [524288, 512], P(('grp', 'row')), may hold values from 0 to 1
- degrees: int32 [524288], P(('grp', 'row')), may hold values from 1024 to 2047
Outputs:
- hidden: bfloat16 [524288, 256], P(('grp', 'row'))
- grad_features: bfloat16 [524288, 256], P(('grp', 'row'))
- grad_self: float32 [256, 256], replicated
- grad_neighbor: float32 [256, 256], replicated
Inputs may be any that keep to these rules, and one draw needn't show every extreme that they name: `send_rows`: rows may repeat.
All inputs are finite; a program needn't handle non-finite values.
Results may differ from a plain program's by a relative error of at most 0.014.
Values may be sent and summed in bfloat16 or wider, within the bound.
A program may use at most 128 MiB of HBM per device.

v0:
```python
import jax
import jax.numpy as jnp
from jax import lax
from jax.sharding import PartitionSpec as P

TILE = 128
HUB = 128


def spread(value, axis, root):
    mine = lax.axis_index(axis) == root
    return lax.psum(jnp.where(mine, value, jnp.zeros_like(value)), axis)


def on_device(
    features,
    cotangent,
    self_weight,
    neighbor_weight,
    tile_values,
    tile_index,
    hub_adjacency,
    hub_owner,
    send_rows,
    cut_adjacency,
    degrees,
):
    node_count, width = features.shape
    tile_total = node_count // TILE
    group_count = lax.axis_size("grp")
    section_count = hub_owner.shape[1]
    values = tile_values[0]
    index = tile_index[0]
    owners = hub_owner[0]
    blocks = features.reshape(tile_total, TILE, width)
    row_select = (index[:, 0][None, :] == jnp.arange(tile_total)[:, None]).astype(jnp.float32)
    col_select = (index[:, 1][None, :] == jnp.arange(tile_total)[:, None]).astype(jnp.float32)
    picked = blocks[index[:, 1]]
    product = jnp.einsum("lab,lbf->laf", values, picked, preferred_element_type=jnp.float32)
    local_sum = jnp.einsum(
        "nl,laf->naf", row_select, product, precision=lax.Precision.HIGHEST
    ).reshape(node_count, width)
    heads = features[:HUB]
    hub_sum = jnp.zeros((node_count, width), jnp.float32)
    for section in range(section_count):
        panel = spread(heads, "row", owners[section])
        hub_sum = hub_sum + jnp.dot(
            hub_adjacency[:, section * HUB : (section + 1) * HUB],
            panel,
            preferred_element_type=jnp.float32,
        )
    outgoing = features[send_rows[0]]
    arrived = lax.all_to_all(outgoing, "grp", split_axis=0, concat_axis=0, tiled=True)
    cut_sum = jnp.dot(
        cut_adjacency,
        arrived.reshape(group_count * outgoing.shape[1], width),
        preferred_element_type=jnp.float32,
    )
    scaling = lax.rsqrt(degrees.astype(jnp.float32))[:, None]
    aggregated = ((local_sum + hub_sum + cut_sum) * scaling).astype(jnp.bfloat16)
    before = jnp.dot(features, self_weight, preferred_element_type=jnp.float32) + jnp.dot(
        aggregated, neighbor_weight, preferred_element_type=jnp.float32
    )
    activated, pullback = jax.vjp(jax.nn.gelu, before)
    hidden = activated.astype(jnp.bfloat16)
    grad_before = pullback(cotangent.astype(jnp.float32))[0].astype(jnp.bfloat16)
    rows_dims = (((0,), (0,)), ((), ()))
    cols_dims = (((1,), (1,)), ((), ()))
    self_part = lax.dot_general(
        features, grad_before, rows_dims, preferred_element_type=jnp.float32
    )
    neighbor_part = lax.dot_general(
        aggregated, grad_before, rows_dims, preferred_element_type=jnp.float32
    )
    grad_self, grad_neighbor = lax.psum((self_part, neighbor_part), ("grp", "row"))
    grad_aggregate = (
        lax.dot_general(grad_before, neighbor_weight, cols_dims, preferred_element_type=jnp.float32)
        * scaling
    ).astype(jnp.bfloat16)
    grad_total = lax.dot_general(
        grad_before, self_weight, cols_dims, preferred_element_type=jnp.float32
    )
    agg_blocks = grad_aggregate.reshape(tile_total, TILE, width)[index[:, 0]]
    returned = jnp.einsum("lab,laf->lbf", values, agg_blocks, preferred_element_type=jnp.float32)
    grad_total = grad_total + jnp.einsum(
        "nl,lbf->nbf", col_select, returned, precision=lax.Precision.HIGHEST
    ).reshape(node_count, width)
    hub_terms = lax.dot_general(
        hub_adjacency, grad_aggregate, rows_dims, preferred_element_type=jnp.float32
    ).reshape(section_count, HUB, width)
    totals = lax.psum(hub_terms.astype(jnp.bfloat16), "row").astype(jnp.float32)
    owned = (owners == lax.axis_index("row")).astype(jnp.float32)
    hub_grad = jnp.einsum("s,shf->hf", owned, totals, precision=lax.Precision.HIGHEST)
    grad_total = grad_total.at[:HUB].add(hub_grad)
    back_rows = lax.dot_general(
        cut_adjacency, grad_aggregate, rows_dims, preferred_element_type=jnp.float32
    ).astype(jnp.bfloat16)
    back_rows = back_rows.reshape(group_count, -1, width)
    returned_rows = lax.all_to_all(back_rows, "grp", split_axis=0, concat_axis=0, tiled=True)
    scatter_table = (send_rows[0].reshape(-1)[None, :] == jnp.arange(node_count)[:, None]).astype(
        jnp.bfloat16
    )
    grad_total = grad_total + jnp.dot(
        scatter_table, returned_rows.reshape(-1, width), preferred_element_type=jnp.float32
    )
    return (hidden, grad_total.astype(jnp.bfloat16), grad_self, grad_neighbor)


def solution(mesh):
    in_specs = (
        P(("grp", "row"), None),
        P(("grp", "row"), None),
        P(),
        P(),
        P(("grp", "row"), None, None, None),
        P(("grp", "row"), None, None),
        P(("grp", "row"), None),
        P("grp", None),
        P(("grp", "row"), None, None),
        P(("grp", "row"), None),
        P(("grp", "row")),
    )
    out_specs = (P(("grp", "row"), None), P(("grp", "row"), None), P(), P())
    return jax.shard_map(
        on_device, mesh=mesh, in_specs=in_specs, out_specs=out_specs, check_vma=False
    )
```

profile of v0, /device:TPU:8, one launch (start us, length us, event | category | flops | bytes accessed | tf_op | source)
XLA Modules:
  0.0 638.3 jit_solution(11707294678581093016)
XLA Ops:
  8.2 3.6 gather_fusion.1
  11.7 5.5 all-to-all-start
  25.0 2.8 gather_fusion
  27.8 6.8 %fusion.25 = f32[64,256,128]{2,1,0:T(8,128)} fusion(bf16[64,128,256]{2,1,0:T(8,128)(2,1)} %gather_fusion, bf16[1,64,128,128]{3,2,1,0:T(8,128)(2,1)S(1)} %copy-done), kind=kOutput, calls=%fused_computation.44 | convolution fusion | flops 536870912 | bytes 14680064 | tf_op jit(solution)/shard_map/lab,lbf->laf/dot_general | solution.py:39
  34.6 9.2 %copy.25 = f32[64,256,128]{1,0,2:T(8,128)} copy(f32[64,256,128]{2,1,0:T(8,128)} %fusion.25) | data formatting | bytes 16777216 | tf_op jit(solution)/shard_map/lab,lbf->laf/dot_general | solution.py:39
  43.8 5.2 fusion.2
  48.9 2.6 copy.18
  51.5 2.9 copy.19
  55.2 1.8 fusion.53
  57.0 117.7 %all-reduce.10.cloned.1.call-done = (bf16[128,256]{1,0:T(8,128)(2,1)}, bf16[128,256]{1,0:T(8,128)(2,1)}, bf16[128,256]{1,0:T(8,128)(2,1)}, bf16[128,256]{1,0:T(8...) async-done(((bf16[128,256]{1,0:T(8,128)(2,1)}, bf16[128,256]{1,0:T(8,128)(2,1)}, ...) | async-done | bytes 524304 | tf_op jit(solution)/shard_map/psum | solution.py:12
  174.6 1.6 fusion.37
  176.2 1.6 convolution_add_fusion.8
  183.5 1.8 fusion.9
  185.4 3.1 fusion.10
  188.5 3.0 fusion.15
  193.9 2.7 fusion.12
  196.5 1.7 copy.29
  198.2 2.8 gather_fusion.2
  201.0 6.8 %fusion.23 = f32[64,256,128]{2,1,0:T(8,128)} fusion(bf16[64,128,256]{2,1,0:T(8,128)(2,1)} %gather_fusion.2, bf16[1,64,128,128]{3,2,1,0:T(8,128)(2,1)S(1)} %copy-done), kind=kOutput, calls=%fused_computation.42 | convolution fusion | flops 536870912 | bytes 14680064 | tf_op jit(solution)/shard_map/lab,laf->lbf/dot_general | solution.py:84
  207.8 9.2 %copy.27 = f32[64,256,128]{1,0,2:T(8,128)} copy(f32[64,256,128]{2,1,0:T(8,128)} %fusion.23) | data formatting | bytes 16777216 | tf_op jit(solution)/shard_map/lab,laf->lbf/dot_general | solution.py:84
  217.0 5.2 fusion
  222.2 2.6 copy.22
  224.8 3.4 fusion.28
  229.2 2.7 fusion.29
  232.8 4.8 all-to-all-start.1
  237.6 3.4 convolution_add_fusion
  241.0 233.6 %all-reduce.8.cloned.1.call-done = (f32[256,256]{0,1:T(8,128)}, f32[256,256]{1,0:T(8,128)}) async-done(((f32[256,256]{0,1:T(8,128)}, f32[256,256]{1,0:T(8,128)}), (f32[256,256]{0,1:T(8,128)}, f32[256,256]{1,0:T(8,128)})) %all-reduce.8.cloned.1.call-update) | async-done | bytes 524304 | tf_op jit(solution)/shard_map/psum | solution.py:75
  474.6 1.8 copy.24
  476.4 148.1 %all-reduce.6.cloned.1.call-done = bf16[8,128,256]{1,0,2:T(8,128)(2,1)} async-done(((bf16[8,128,256]{1,0,2:T(8,128)(2,1)}), bf16[8,128,256]{1,0,2:T(8,128)(2,1)}) %all-reduce.6.cloned.1.call-update) | async-done | bytes 524304 | tf_op jit(solution)/shard_map/psum | solution.py:91
  624.6 1.3 fusion.46
  626.0 1.6 fusion.39
  627.6 3.4 fusion.11
  (78 shorter events, 15.0 us)
Async XLA Ops:
  7.2 20.6 %copy-start = (bf16[1,64,128,128]{3,2,1,0:T(8,128)(2,1)S(1)}, bf16[1,64,128,128]{3,2,1,0:T(8,128)(2,1)}, u32[]{:S(2)}) copy-start(bf16[1,64,128,128]{3,2,1,0:T(8,128)(2,1)} %param.17) | copy-start | bytes 6291460
  7.2 16.6 %copy-start.20 = (s32[1,8,64]{2,1,0:T(8,128)S(1)}, s32[1,8,64]{2,1,0:T(8,128)}, u32[]{:S(2)}) copy-start(s32[1,8,64]{2,1,0:T(8,128)} %param.21) | copy-start | bytes 6148
  7.2 15.7 %copy-start.1 = (bf16[2048,256]{1,0:T(8,128)(2,1)S(1)}, bf16[2048,256]{1,0:T(8,128)(2,1)}, u32[]{:S(2)}) copy-start(bf16[2048,256]{1,0:T(8,128)(2,1)} %param.13) | copy-start | bytes 3145732
  7.2 10.0 %copy-start.19 = (s32[1,8]{1,0:T(1,128)S(1)}, s32[1,8]{1,0:T(1,128)}, u32[]{:S(2)}) copy-start(s32[1,8]{1,0:T(1,128)} %param.20) | copy-start | bytes 100
  7.2 17.2 %copy-start.23 = (s32[1,64,2]{1,2,0:T(2,128)S(1)}, s32[1,64,2]{1,2,0:T(2,128)}, u32[]{:S(2)}) copy-start(s32[1,64,2]{1,2,0:T(2,128)} %param.18) | copy-start | bytes 1540
  11.7 173.6 %all-to-all-start = ((bf16[8,64,256]{2,1,0:T(8,128)(2,1)}), bf16[8,64,256]{2,1,0:T(8,128)(2,1)S(1)}, u32[]{:S(2)}, u32[]{:S(2)}) async-start(bf16[8,64,256]{2,1,0:T(8,128)(2,1)} %bitcast.18), calls=%async_computation | async-start | bytes 524288 | tf_op jit(solution)/shard_map/all_to_all | solution.py:53
  17.2 157.4 %all-reduce.10.cloned.1.call-start = ((), (), s32[]{:S(2)}) async-start(), calls=%async_computation.4 | async-start | bytes 1048576 | tf_op jit(solution)/shard_map/psum | solution.py:12
  23.7 450.9 %all-reduce.8.cloned.1.call-start = ((), (), s32[]{:S(2)}) async-start(), calls=%async_computation.3 | async-start | bytes 1048576 | tf_op jit(solution)/shard_map/psum | solution.py:75
  51.5 3.6 copy-start.8
  174.6 1.6 copy-start.18
  176.2 2.4 copy-start.5
  176.2 2.4 copy-start.17
  178.6 0.8 copy-start.16
  179.4 0.8 copy-start.15
  180.3 0.8 copy-start.14
  181.1 0.8 copy-start.13
  182.0 1.6 copy-start.4
  182.0 1.6 copy-start.12
  185.3 3.2 copy-start.7
  185.4 3.2 copy-start.10
  185.4 3.2 copy-start.24
  191.5 1.1 copy-start.2
  191.5 2.3 copy-start.11
  207.8 9.2 %copy-start.22 = (s32[64]{0:T(128)S(1)}, s32[64]{0:T(128)}, u32[]{:S(2)}) copy-start(s32[64]{0:T(128)} %get-tuple-element.44) | copy-start | bytes 772
  222.2 2.7 copy-start.6
  224.8 399.8 %all-reduce.6.cloned.1.call-start = ((), (), s32[]{:S(2)}) async-start(), calls=%async_computation.2 | async-start | bytes 1048576 | tf_op jit(solution)/shard_map/psum | solution.py:91
  229.2 8.4 %copy-start.3 = (bf16[2048,256]{1,0:T(8,128)(2,1)S(1)}, bf16[2048,256]{1,0:T(8,128)(2,1)}, u32[]{:S(2)}) copy-start(bf16[2048,256]{1,0:T(8,128)(2,1)} %copy-done.2) | copy-start | bytes 3145732
  232.8 394.9 %all-to-all-start.1 = ((bf16[8,64,256]{2,1,0:T(8,128)(2,1)}), bf16[8,64,256]{2,1,0:T(8,128)(2,1)S(1)}, u32[]{:S(2)}, u32[]{:S(2)}) async-start(bf16[8,64,256]{2,1,0:T(8,128)(2,1)} %bitcast.32), calls=%async_computation.1 | async-start | bytes 524288 | tf_op jit(solution)/shard_map/all_to_all | solution.py:99
  237.6 390.0 %copy-start.21 = (s32[512]{0:T(512)S(1)}, s32[512]{0:T(512)}, u32[]{:S(2)}) copy-start(s32[512]{0:T(512)} %eq.97) | copy-start | bytes 6148
  626.0 5.1 copy-start.9
Sparse Core Ops, SparseCore 0:
  23.8 150.7 all-reduce.9
  224.9 249.6 all-reduce.7
  478.4 146.1 all-reduce.5
where the time goes:
time: 640 us; the launch traced here: 638 us
  waiting for transfers between devices  499 us (78%)
  matrix products  58.4 us (9%)
  local copies, waits for them, and re-layouts  46.5 us (7%)
  between operations  19 us (3%)
  starting transfers between devices  10.4 us (2%)
    psum x1, waiting for transfers between devices, on_device(): lax.psum((self_part, neighbor_part), ('grp', 'row'))  234 us
    psum x1, waiting for transfers between devices, on_device(): totals = lax.psum(hub_terms.astype(jnp.bfloat16), 'row').astype(jnp.float32)  148 us
    psum x1, waiting for transfers between devices, spread(): return lax.psum(jnp.where(mine, value, jnp.zeros_like(value)), axis)  118 us
  transfers between devices with their start and end apart: 5, of which 3 were waited for; matrix products, arithmetic and copies ran while one was open for 9% of the time, Pallas kernels for 0%

commit v1 on v0

--- a/solution.py
+++ b/solution.py
@@ -2,14 +2,20 @@
 import jax.numpy as jnp
 from jax import lax
 from jax.sharding import PartitionSpec as P
+from jax.lax import all_gather
 
 TILE = 128
 HUB = 128
 
 
+def post_run(page, ax_name):
+    shaped = all_gather(page, axis_name=ax_name)
+    return jnp.sum(shaped, 0)
+
+
 def spread(value, axis, root):
     mine = lax.axis_index(axis) == root
-    return lax.psum(jnp.where(mine, value, jnp.zeros_like(value)), axis)
+    return post_run(jnp.where(mine, value, jnp.zeros_like(value)), axis)
 
 
 def on_device(

time: 640 us -> 1110 us (1.73)
  waiting for transfers between devices: 499 us -> 948 us
  other arithmetic: 4.54 us -> 25.3 us
    all_gather x0 -> x8, waiting for transfers between devices: none -> 562 us  [post_run(): shaped = all_gather(page, axis_name=ax_name)]
    psum x1 -> x0, waiting for transfers between devices: 118 us -> none  [spread(): return lax.psum(jnp.where(mine, value, jnp.zeros_like(value)), axis)]
    reduce_sum x0 -> x8, other arithmetic: none -> 20.1 us  [post_run(): return jnp.sum(shaped, 0)]
  transfers between devices with their start and end apart: 5 -> 12, of which waited for: 3 -> 10; matrix products, arithmetic and copies ran while one was open for 9% -> 7% of each run, Pallas kernels for 0% -> 0%
where the time goes in v1:
time: 1110 us
  waiting for transfers between devices  948 us (85%)
  matrix products  58.4 us (5%)
  local copies, waits for them, and re-layouts  46.5 us (4%)
  other arithmetic  25.3 us (2%)
  between operations  19.5 us (2%)
    all_gather x8, waiting for transfers between devices, post_run(): shaped = all_gather(page, axis_name=ax_name)  562 us
    psum x1, waiting for transfers between devices, on_device(): lax.psum((self_part, neighbor_part), ('grp', 'row'))  234 us
    psum x1, waiting for transfers between devices, on_device(): totals = lax.psum(hub_terms.astype(jnp.bfloat16), 'row').astype(jnp.float32)  148 us
  transfers between devices with their start and end apart: 12, of which 10 were waited for; matrix products, arithmetic and copies ran while one was open for 7% of the time, Pallas kernels for 0%

profile of v1, /device:TPU:8, one launch (start us, length us, event | category | flops | bytes accessed | tf_op | source)
XLA Modules:
  0.0 1108.1 jit_solution(2156423151268111163)
XLA Ops:
  21.1 2.6 gather_fusion.1
  23.7 5.5 all-to-all-start
  31.0 2.8 gather_fusion
  33.8 6.8 fusion.25
  40.6 9.2 copy.25
  49.8 5.2 fusion.2
  54.9 2.6 copy.18
  57.5 2.9 copy.19
  62.3 34.2 %all-gather.17.cloned.1.call-done = bf16[4096,256]{1,0:T(8,128)(2,1)} async-done(((bf16[128,256]{1,0:T(8,128)(2,1)}), bf16[4096,256]{1,0:T(8,128)(2,1)}) %all-gather.17.cloned.1.call-update) | async-done | bytes 2097168 | tf_op jit(solution)/shard_map/all_gather | solution.py:12
  99.0 75.8 %all-gather.19.cloned.1.call-done = bf16[4096,256]{1,0:T(8,128)(2,1)} async-done(((bf16[128,256]{1,0:T(8,128)(2,1)}), bf16[4096,256]{1,0:T(8,128)(2,1)}) %all-gather.19.cloned.1.call-update) | async-done | bytes 2097168 | tf_op jit(solution)/shard_map/all_gather | solution.py:12
  177.3 75.8 %all-gather.21.cloned.1.call-done = bf16[4096,256]{1,0:T(8,128)(2,1)} async-done(((bf16[128,256]{1,0:T(8,128)(2,1)}), bf16[4096,256]{1,0:T(8,128)(2,1)}) %all-gather.21.cloned.1.call-update) | async-done | bytes 2097168 | tf_op jit(solution)/shard_map/all_gather | solution.py:12
  255.7 75.1 %all-gather.23.cloned.1.call-done = bf16[4096,256]{1,0:T(8,128)(2,1)} async-done(((bf16[128,256]{1,0:T(8,128)(2,1)}), bf16[4096,256]{1,0:T(8,128)(2,1)}) %all-gather.23.cloned.1.call-update) | async-done | bytes 2097168 | tf_op jit(solution)/shard_map/all_gather | solution.py:12
  330.7 2.5 reduce_sum.99
  333.2 75.1 %all-gather.25.cloned.1.call-done = bf16[4096,256]{1,0:T(8,128)(2,1)} async-done(((bf16[128,256]{1,0:T(8,128)(2,1)}), bf16[4096,256]{1,0:T(8,128)(2,1)}) %all-gather.25.cloned.1.call-update) | async-done | bytes 2097168 | tf_op jit(solution)/shard_map/all_gather | solution.py:12
  410.8 75.1 %all-gather.27.cloned.1.call-done = bf16[4096,256]{1,0:T(8,128)(2,1)} async-done(((bf16[128,256]{1,0:T(8,128)(2,1)}), bf16[4096,256]{1,0:T(8,128)(2,1)}) %all-gather.27.cloned.1.call-update) | async-done | bytes 2097168 | tf_op jit(solution)/shard_map/all_gather | solution.py:12
  488.4 75.2 %all-gather.29.cloned.1.call-done = bf16[4096,256]{1,0:T(8,128)(2,1)} async-done(((bf16[128,256]{1,0:T(8,128)(2,1)}), bf16[4096,256]{1,0:T(8,128)(2,1)}) %all-gather.29.cloned.1.call-update) | async-done | bytes 2097168 | tf_op jit(solution)/shard_map/all_gather | solution.py:12
  566.1 75.8 %all-gather.31.cloned.1.call-done = bf16[4096,256]{1,0:T(8,128)(2,1)} async-done(((bf16[128,256]{1,0:T(8,128)(2,1)}), bf16[4096,256]{1,0:T(8,128)(2,1)}) %all-gather.31.cloned.1.call-update) | async-done | bytes 2097168 | tf_op jit(solution)/shard_map/all_gather | solution.py:12
  655.2 3.1 fusion.10
  658.4 3.0 fusion.15
  663.7 2.7 fusion.12
  668.1 2.9 gather_fusion.2
  671.0 6.8 fusion.23
  677.8 9.2 copy.27
  686.9 5.2 fusion
  692.1 2.6 copy.22
  694.8 3.4 fusion.28
  699.2 2.7 fusion.29
  702.7 4.8 all-to-all-start.1
  707.6 3.4 convolution_add_fusion
  711.0 233.7 %all-reduce.6.cloned.1.call-done = (f32[256,256]{0,1:T(8,128)}, f32[256,256]{1,0:T(8,128)}) async-done(((f32[256,256]{0,1:T(8,128)}, f32[256,256]{1,0:T(8,128)}), (f32[256,256]{0,1:T(8,128)}, f32[256,256]{1,0:T(8,128)})) %all-reduce.6.cloned.1.call-update) | async-done | bytes 524304 | tf_op jit(solution)/shard_map/psum | solution.py:81
  946.5 147.6 %all-reduce.4.cloned.1.call-done = bf16[8,128,256]{1,0,2:T(8,128)(2,1)} async-done(((bf16[8,128,256]{1,0,2:T(8,128)(2,1)}), bf16[8,128,256]{1,0,2:T(8,128)(2,1)}) %all-reduce.4.cloned.1.call-update) | async-done | bytes 524304 | tf_op jit(solution)/shard_map/psum | solution.py:97
  1097.1 3.4 fusion.11
  (109 shorter events, 52.0 us)
Async XLA Ops:
  7.2 26.7 %copy-start = (bf16[1,64,128,128]{3,2,1,0:T(8,128)(2,1)S(1)}, bf16[1,64,128,128]{3,2,1,0:T(8,128)(2,1)}, u32[]{:S(2)}) copy-start(bf16[1,64,128,128]{3,2,1,0:T(8,128)(2,1)} %param.17) | copy-start | bytes 6291460
  7.2 13.9 %copy-start.1 = (bf16[2048,256]{1,0:T(8,128)(2,1)S(1)}, bf16[2048,256]{1,0:T(8,128)(2,1)}, u32[]{:S(2)}) copy-start(bf16[2048,256]{1,0:T(8,128)(2,1)} %param.13) | copy-start | bytes 3145732
  7.2 22.0 %copy-start.20 = (s32[1,8,64]{2,1,0:T(8,128)S(1)}, s32[1,8,64]{2,1,0:T(8,128)}, u32[]{:S(2)}) copy-start(s32[1,8,64]{2,1,0:T(8,128)} %param.21) | copy-start | bytes 6148
  7.2 22.6 %copy-start.24 = (s32[1,64,2]{1,2,0:T(2,128)S(1)}, s32[1,64,2]{1,2,0:T(2,128)}, u32[]{:S(2)}) copy-start(s32[1,64,2]{1,2,0:T(2,128)} %param.18) | copy-start | bytes 1540
  7.2 89.3 %all-gather.17.cloned.1.call-start = ((), (), s32[]{:S(2)}) async-start(), calls=%async_computation.3 | async-start | bytes 2162688 | tf_op jit(solution)/shard_map/all_gather | solution.py:12
  15.6 159.2 %all-gather.19.cloned.1.call-start = ((), (), s32[]{:S(2)}) async-start(), calls=%async_computation.4 | async-start | bytes 2162688 | tf_op jit(solution)/shard_map/all_gather | solution.py:12
  16.4 236.8 %all-gather.21.cloned.1.call-start = ((), (), s32[]{:S(2)}) async-start(), calls=%async_computation.5 | async-start | bytes 2162688 | tf_op jit(solution)/shard_map/all_gather | solution.py:12
  17.1 313.6 %all-gather.23.cloned.1.call-start = ((), (), s32[]{:S(2)}) async-start(), calls=%async_computation.6 | async-start | bytes 2162688 | tf_op jit(solution)/shard_map/all_gather | solution.py:12
  17.7 390.6 %all-gather.25.cloned.1.call-start = ((), (), s32[]{:S(2)}) async-start(), calls=%async_computation.7 | async-start | bytes 2162688 | tf_op jit(solution)/shard_map/all_gather | solution.py:12
  18.3 467.6 %all-gather.27.cloned.1.call-start = ((), (), s32[]{:S(2)}) async-start(), calls=%async_computation.8 | async-start | bytes 2162688 | tf_op jit(solution)/shard_map/all_gather | solution.py:12
  18.8 544.8 %all-gather.29.cloned.1.call-start = ((), (), s32[]{:S(2)}) async-start(), calls=%async_computation.9 | async-start | bytes 2162688 | tf_op jit(solution)/shard_map/all_gather | solution.py:12
  19.6 622.3 %all-gather.31.cloned.1.call-start = ((), (), s32[]{:S(2)}) async-start(), calls=%async_computation.10 | async-start | bytes 2162688 | tf_op jit(solution)/shard_map/all_gather | solution.py:12
  23.7 631.5 %all-to-all-start = ((bf16[8,64,256]{2,1,0:T(8,128)(2,1)}), bf16[8,64,256]{2,1,0:T(8,128)(2,1)S(1)}, u32[]{:S(2)}, u32[]{:S(2)}) async-start(bf16[8,64,256]{2,1,0:T(8,128)(2,1)} %bitcast.26), calls=%async_computation | async-start | bytes 524288 | tf_op jit(solution)/shard_map/all_to_all | solution.py:59
  29.2 915.5 %all-reduce.6.cloned.1.call-start = ((), (), s32[]{:S(2)}) async-start(), calls=%async_computation.11 | async-start | bytes 1048576 | tf_op jit(solution)/shard_map/psum | solution.py:81
  57.5 2.9 copy-start.21
  57.5 3.0 copy-start.8
  646.0 2.4 copy-start.5
  646.1 2.4 copy-start.10
  651.8 1.6 copy-start.4
  651.8 1.6 copy-start.15
  655.2 3.2 copy-start.7
  655.2 3.2 copy-start.17
  655.2 3.2 copy-start.25
  661.4 2.3 copy-start.18
  677.7 9.2 copy-start.23
  692.1 2.7 copy-start.6
  694.7 399.4 %all-reduce.4.cloned.1.call-start = ((), (), s32[]{:S(2)}) async-start(), calls=%async_computation.2 | async-start | bytes 1048576 | tf_op jit(solution)/shard_map/psum | solution.py:97
  699.1 8.4 copy-start.3
  702.7 394.4 %all-to-all-start.1 = ((bf16[8,64,256]{2,1,0:T(8,128)(2,1)}), bf16[8,64,256]{2,1,0:T(8,128)(2,1)S(1)}, u32[]{:S(2)}, u32[]{:S(2)}) async-start(bf16[8,64,256]{2,1,0:T(8,128)(2,1)} %bitcast.40), calls=%async_computation.1 | async-start | bytes 524288 | tf_op jit(solution)/shard_map/all_to_all | solution.py:105
  707.5 386.5 %copy-start.19 = (s32[1,8]{1,0:T(1,128)S(1)}, s32[1,8]{1,0:T(1,128)}, u32[]{:S(2)}) copy-start(s32[1,8]{1,0:T(1,128)} %param.20) | copy-start | bytes 100
  707.5 389.6 %copy-start.22 = (s32[512]{0:T(512)S(1)}, s32[512]{0:T(512)}, u32[]{:S(2)}) copy-start(s32[512]{0:T(512)} %eq.97) | copy-start | bytes 6148
  1095.5 5.1 copy-start.16
  (6 other events, 6.1 us)
Sparse Core Ops, SparseCore 0:
  15.7 80.7 all-gather.16
  99.7 75.1 all-gather.18
  178.0 75.1 all-gather.20
  255.6 75.1 all-gather.22
  333.2 75.1 all-gather.24
  410.7 75.1 all-gather.26
  488.5 75.1 all-gather.28
  566.8 75.1 all-gather.30
  694.8 249.7 all-reduce.5
  947.9 146.1 all-reduce.3
